TPU v7x, 256 devices: a whole 4x4x8 slice. The times are simulated.
256 devices in a mesh: dp: 64 (over y, z, core), rep: 4 (over x).
Axes of the slice: x: 4, y: 4, z: 8, core: 2. Of those that a mesh axis runs over, the one named last changes fastest.
Arguments:
- item_table: bfloat16 [32768, 512], P(('dp', 'rep')), may hold values from -6 to 6
- requests: int32 [256, 256, 2], P(('dp', 'rep')), may hold values from 0 to 127, as said below
- event_slot: int32 [131072], P(('dp', 'rep')), may hold values from 0 to 511, as said below
- lengths: int32 [256, 4], P(('dp', 'rep')), may hold values from 1 to 256, 512 in all within a row
- leaf_ids: int32 [131072, 8], P(('dp', 'rep')), may hold values from 0 to 31
- leaf_table: bfloat16 [256, 512], replicated, may hold values from -2.09375 to 2.09375
- w_in: bfloat16 [512, 2048], replicated, may hold values from -0.25 to 0.25
- w_out: bfloat16 [512, 512], replicated, may hold values from -0.25 to 0.25
- cotangent: bfloat16 [131072, 512], P(('dp', 'rep')), may hold values from -6 to 6
Outputs:
- output: bfloat16 [131072, 512], P(('dp', 'rep'))
- table_grad: float32 [32768, 512], P(('dp', 'rep'))
- leaf_grad: float32 [256, 512], replicated
- w_in_grad: float32 [512, 2048], replicated
- w_out_grad: float32 [512, 512], replicated
Inputs may be any that keep to these rules, and one draw needn't show every extreme that they name: `requests`: for each device and owner the 2 requested rows are distinct. `event_slot`: every one of a device's 512 slots is named by at least one of its events.
All inputs are finite; a program needn't handle non-finite values.
Results may differ from a plain program's by a relative error of at most 0.014.
Values may be sent and summed in bfloat16 or wider, within the bound.
A program may use at most 64 MiB of HBM per device.

v0:
```python
import jax
import jax.numpy as jnp
from jax import lax
from jax.sharding import PartitionSpec as P

HEADS = 4
epsilon = 1e-06


def normalize(values):
    center = values - jnp.mean(values, axis=-1, keepdims=True)
    spread = jnp.mean(center * center, axis=-1, keepdims=True)
    return center * lax.rsqrt(spread + epsilon)


def visible(lengths, count):
    ends = jnp.cumsum(lengths)
    places = jnp.arange(count, dtype=jnp.int32)
    segment = jnp.sum((places[:, None] >= ends[None, :]).astype(jnp.int32), axis=1)
    same = segment[:, None] == segment[None, :]
    return jnp.logical_and(same, places[None, :] <= places[:, None])


def front(rows, event_slot, lengths, leaf_ids, leaf_table, w_in):
    count = event_slot.shape[0]
    picker = (event_slot[:, None] == jnp.arange(rows.shape[0], dtype=jnp.int32)[None, :]).astype(
        jnp.bfloat16
    )
    leaves = leaf_table.shape[0] // leaf_ids.shape[1]
    onehot = (
        (leaf_ids[:, :, None] == jnp.arange(leaves, dtype=jnp.int32)[None, None, :])
        .reshape(count, -1)
        .astype(jnp.bfloat16)
    )
    inputs = (
        jnp.dot(picker, rows, preferred_element_type=jnp.float32)
        + jnp.dot(onehot, leaf_table, preferred_element_type=jnp.float32)
    ).astype(jnp.bfloat16)
    normed = normalize(inputs.astype(jnp.float32)).astype(jnp.bfloat16)
    hidden = jax.nn.silu(jnp.dot(normed, w_in, preferred_element_type=jnp.float32)).astype(
        jnp.bfloat16
    )
    width = w_in.shape[0]
    head_size = width // HEADS
    gates = hidden[:, 0:width]
    value_heads = hidden[:, width : 2 * width].reshape(count, HEADS, head_size)
    query_heads = hidden[:, 2 * width : 3 * width].reshape(count, HEADS, head_size)
    key_heads = hidden[:, 3 * width : 4 * width].reshape(count, HEADS, head_size)
    scores = jnp.einsum(
        "qhd,khd->hqk", query_heads, key_heads, preferred_element_type=jnp.float32
    ) * head_size ** (-0.5)
    allowed = visible(lengths, count)
    weights = jnp.where(allowed[None], jax.nn.silu(scores), 0.0).astype(jnp.bfloat16)
    mixed = jnp.einsum(
        "hqk,khd->qhd", weights, value_heads, preferred_element_type=jnp.float32
    ).reshape(count, width)
    gated = (normalize(mixed) * gates.astype(jnp.float32)).astype(jnp.bfloat16)
    return (inputs, gated)


def back(inputs, gated, w_out):
    return (
        jnp.dot(gated, w_out, preferred_element_type=jnp.float32) + inputs.astype(jnp.float32)
    ).astype(jnp.bfloat16)


def send_asked(wanted):
    result = lax.all_to_all(
        lax.all_to_all(wanted, "dp", split_axis=0, concat_axis=0, tiled=True),
        "rep",
        split_axis=1,
        concat_axis=1,
        tiled=True,
    )
    return result


def send_fetched(fetched):
    result = lax.all_to_all(
        lax.all_to_all(fetched, "dp", split_axis=0, concat_axis=0, tiled=True),
        "rep",
        split_axis=1,
        concat_axis=1,
        tiled=True,
    )
    return result


def send_returned(gradients):
    result = lax.all_to_all(
        lax.all_to_all(gradients, "dp", split_axis=0, concat_axis=0, tiled=True),
        "rep",
        split_axis=1,
        concat_axis=1,
        tiled=True,
    )
    return result


def on_device(
    item_table, requests, event_slot, lengths, leaf_ids, leaf_table, w_in, w_out, cotangent
):
    data_count = lax.axis_size("dp")
    replica_count = lax.axis_size("rep")
    width = item_table.shape[1]
    wanted = requests.reshape(data_count, replica_count, -1)
    asked = send_asked(wanted)
    fetched = item_table[asked]
    arrived = send_fetched(fetched).reshape(-1, width)

    def local_front(rows, table_leaf, weight_in):
        return front(rows, event_slot, lengths[0], leaf_ids, table_leaf, weight_in)

    (inputs, gated), pull_front = jax.vjp(local_front, arrived, leaf_table, w_in)
    output, pull_back = jax.vjp(back, inputs, gated, w_out)
    d_inputs, d_gated, d_out = pull_back(cotangent)
    d_rows, d_leaf, d_in = pull_front((d_inputs, d_gated))
    returned = send_returned(d_rows.reshape(data_count, replica_count, -1, width))
    leaf_sum, in_sum, out_sum = lax.psum(
        (d_leaf.astype(jnp.float32), d_in.astype(jnp.float32), d_out.astype(jnp.float32)),
        ("dp", "rep"),
    )
    table_grad = (
        jnp.zeros(item_table.shape, jnp.float32)
        .at[asked.reshape(-1)]
        .add(returned.reshape(-1, width).astype(jnp.float32))
    )
    share = 1.0 / (data_count * replica_count)
    return (output, table_grad, leaf_sum * share, in_sum * share, out_sum * share)


def solution(mesh):
    return jax.shard_map(
        on_device,
        mesh=mesh,
        in_specs=(
            P(("dp", "rep"), None),
            P(("dp", "rep"), None, None),
            P(("dp", "rep")),
            P(("dp", "rep"), None),
            P(("dp", "rep"), None),
            P(),
            P(),
            P(),
            P(("dp", "rep"), None),
        ),
        out_specs=(P(("dp", "rep"), None), P(("dp", "rep"), None), P(), P(), P()),
        check_vma=False,
    )
```

profile of v0, /device:TPU:97, one launch (start us, length us, event | category | flops | bytes accessed | tf_op | source)
XLA Modules:
  0.0 433.1 jit_solution(8049075674224172676)
XLA Ops:
  8.2 18.3 %all_to_all.30 = s32[64,4,2]{1,2,0:T(2,128)S(1)} all-to-all(s32[64,4,2]{1,2,0:T(2,128)S(1)} %copy.143), channel_id=1, replica_groups=mesh['dp'=64,'rep'=4] {'dp'}, dimensions={0} | all-to-all | bytes 4096 | tf_op jit(solution)/shard_map/all_to_all | solution.py:69
  26.7 7.9 %all_to_all.31 = s32[4,1,128]{2,1,0:T(1,128)S(1)} all-to-all(s32[4,1,128]{2,1,0:T(1,128)S(1)} %reshape.234), channel_id=1, replica_groups=mesh['dp'=64,'rep'=4] {'rep'}, dimensions={0} | all-to-all | bytes 4096 | tf_op jit(solution)/shard_map/all_to_all | solution.py:68
  36.2 2.9 gather_fusion
  40.1 8.5 %all-to-all-start.2 = ((bf16[64,4,2,512]{3,2,1,0:T(2,128)(2,1)}), bf16[64,4,2,512]{3,2,1,0:T(2,128)(2,1)S(1)}, u32[]{:S(2)}, u32[]{:S(2)}) async-start(bf16[64,4,2,512]{3,2,1,0:T(2,128)(2,1)} %reshape.215), calls=%async_computation.2 | async-start | bytes 1048576 | tf_op jit(solution)/shard_map/all_to_all | solution.py:80
  50.1 15.3 %all-to-all-done.2 = bf16[64,4,2,512]{3,2,1,0:T(2,128)(2,1)S(1)} async-done(((bf16[64,4,2,512]{3,2,1,0:T(2,128)(2,1)}), bf16[64,4,2,512]{3,2,1,0:T(2,128)(2,1)S(1)}, u32[]{:S(2)}, u32[]{:S(2)}) %all-to-all-start.2) | async-done | bytes 524320 | tf_op jit(solution)/shard_map/all_to_all | solution.py:80
  66.6 3.5 all-to-all-start.3
  70.5 2.3 fusion.42
  72.8 7.3 %all-to-all-done.3 = bf16[64,4,2,512]{3,2,0,1:T(2,128)(2,1)S(1)} async-done(((bf16[64,4,2,512]{3,2,0,1:T(2,128)(2,1)}), bf16[64,4,2,512]{3,2,0,1:T(2,128)(2,1)S(1)}, u32[]{:S(2)}, u32[]{:S(2)}) %all-to-all-start.3) | async-done | bytes 524320 | tf_op jit(solution)/shard_map/all_to_all | solution.py:79
  86.0 3.9 multiply_convert_fusion
  96.5 4.8 %select_convert_fusion = (bf16[4,512,512]{2,1,0:T(8,128)(2,1)S(1)}, f32[4,512,512]{2,1,0:T(8,128)}) fusion(pred[512,512]{1,0:T(8,128)(4,1)S(1)} %fusion.22, bf16[512,4,128]{0,2,1:T(8,128)(2,1)} %bitcast.68, bf16[512,4,128]{0,2,1:T(8,128)(2,1)} %bitcast.70), kind=kOutput, calls=%fused_computation.11 | convolution fusion | flops 275775488 | bytes 7602176 | tf_op jit(solution)/shard_map/jvp(qhd,khd->hqk)/dot_general | solution.py:49
  103.9 2.6 copy.171
  109.3 3.0 fusion.40
  115.3 5.1 %fusion.4 = bf16[4,512,512]{2,1,0:T(8,128)(2,1)S(1)} fusion(f32[4,512,512]{2,1,0:T(8,128)} %get-tuple-element.57, pred[512,512]{1,0:T(8,128)(4,1)S(1)} %fusion.22, bf16[4,128,512]{2,1,0:T(8,128)(2,1)} %bitcast.72, bf16[64,4,8,128]{3,2,1,0:T(8,128)(2,1)} %get-tuple-element.46), kind=kOutput, calls=%fused_computation.10 | convolution fusion | flops 283115520 | bytes 7602176 | tf_op jit(solution)/shard_map/transpose(jvp(hqk,khd->qhd))/dot_general | solution.py:54
  130.9 3.6 fusion
  134.5 3.3 fusion.5
  143.3 2.5 convolution_convert_fusion.1
  147.9 6.8 %all-to-all-start.4 = ((bf16[64,4,2,512]{3,2,1,0:T(2,128)(2,1)}), bf16[64,4,2,512]{3,2,1,0:T(2,128)(2,1)}, u32[]{:S(2)}, u32[]{:S(2)}) async-start(bf16[64,4,2,512]{3,2,1,0:T(2,128)(2,1)} %reshape.212), calls=%async_computation.4 | async-start | bytes 1048576 | tf_op jit(solution)/shard_map/all_to_all | solution.py:91
  155.0 17.6 %all-to-all-done.4 = bf16[64,4,2,512]{3,2,1,0:T(2,128)(2,1)} async-done(((bf16[64,4,2,512]{3,2,1,0:T(2,128)(2,1)}), bf16[64,4,2,512]{3,2,1,0:T(2,128)(2,1)}, u32[]{:S(2)}, u32[]{:S(2)}) %all-to-all-start.4) | async-done | bytes 524320 | tf_op jit(solution)/shard_map/all_to_all | solution.py:91
  174.8 4.4 %all-to-all-start.5 = ((bf16[64,4,2,512]{3,2,0,1:T(2,128)(2,1)}), bf16[64,4,2,512]{3,2,0,1:T(2,128)(2,1)}, u32[]{:S(2)}, u32[]{:S(2)}) async-start(bf16[64,4,2,512]{3,2,0,1:T(2,128)(2,1)} %copy.164), calls=%async_computation.5 | async-start | bytes 1048576 | tf_op jit(solution)/shard_map/all_to_all | solution.py:90
  179.2 2.3 fusion.11
  183.6 5.3 %all-to-all-done.5 = bf16[64,4,2,512]{3,2,0,1:T(2,128)(2,1)} async-done(((bf16[64,4,2,512]{3,2,0,1:T(2,128)(2,1)}), bf16[64,4,2,512]{3,2,0,1:T(2,128)(2,1)}, u32[]{:S(2)}, u32[]{:S(2)}) %all-to-all-start.5) | async-done | bytes 524320 | tf_op jit(solution)/shard_map/all_to_all | solution.py:90
  192.6 4.9 %scatter_custom_fusion = f32[128,512]{1,0:T(8,128)} fusion(s32[512]{0:T(512)S(1)} %bitcast.79, f32[512,512]{1,0:T(8,128)} %reshape.226, f32[]{:T(128)} %constant.15.clone.1), kind=kCustom, calls=%fused_computation.74 | custom fusion | flops 262144 | bytes 262656 | tf_op jit(solution)/shard_map/scatter-add | solution.py:126
  197.6 221.8 %all-reduce.7.cloned.1.call-done = (f32[256,512]{1,0:T(8,128)}, f32[512,2048]{1,0:T(8,128)}, f32[512,512]{1,0:T(8,128)}) async-done(((f32[256,512]{1,0:T(8,128)}, f32[512,2048]{1,0:T(8,128)}, f32[512,512]{1,0:T(8,128)}), (f32[256,512]{1,0:T(8,128)}, f32[512,2048]{1,0:T(8,128)}, f32[512,512]{1,0:T(8,128)})) %all-reduce.7.cloned.1.call-update) | async-done | bytes 5767184 | tf_op jit(solution)/shard_map/psum | solution.py:119
  419.4 4.9 %broadcast_multiply_fusion = f32[512,2048]{1,0:T(8,128)} fusion(f32[512,2048]{1,0:T(8,128)} %get-tuple-element.41), kind=kLoop, calls=%fused_computation.17 | loop fusion | flops 1048576 | bytes 8388608 | tf_op jit(solution)/shard_map/mul | solution.py:129
  (107 shorter events, 55.9 us)
Async XLA Ops:
  7.2 78.8 %copy-start = (bf16[512,2048]{1,0:T(8,128)(2,1)S(1)}, bf16[512,2048]{1,0:T(8,128)(2,1)}, u32[]{:S(2)}) copy-start(bf16[512,2048]{1,0:T(8,128)(2,1)} %param.15) | copy-start | bytes 6291460
  7.2 41.5 %copy-start.21 = (s32[1,4]{1,0:T(1,128)S(1)}, s32[1,4]{1,0:T(1,128)}, u32[]{:S(2)}) copy-start(s32[1,4]{1,0:T(1,128)} %param.12) | copy-start | bytes 52
  7.2 41.7 %copy-start.4 = (bf16[512,512]{1,0:T(8,128)(2,1)S(1)}, bf16[512,512]{1,0:T(8,128)(2,1)}, u32[]{:S(2)}) copy-start(bf16[512,512]{1,0:T(8,128)(2,1)} %param.17) | copy-start | bytes 1572868
  26.5 23.4 %copy-start.18 = (s32[512,8]{0,1:T(8,128)S(1)}, s32[512,8]{0,1:T(8,128)}, u32[]{:S(2)}) copy-start(s32[512,8]{0,1:T(8,128)} %param.13) | copy-start | bytes 49156
  40.1 43.1 %copy-start.19 = (s32[512]{0:T(512)S(1)}, s32[512]{0:T(512)}, u32[]{:S(2)}) copy-start(s32[512]{0:T(512)} %param.11) | copy-start | bytes 6148
  40.1 25.3 %all-to-all-start.2 = ((bf16[64,4,2,512]{3,2,1,0:T(2,128)(2,1)}), bf16[64,4,2,512]{3,2,1,0:T(2,128)(2,1)S(1)}, u32[]{:S(2)}, u32[]{:S(2)}) async-start(bf16[64,4,2,512]{3,2,1,0:T(2,128)(2,1)} %reshape.215), calls=%async_computation.2 | async-start | bytes 1048576 | tf_op jit(solution)/shard_map/all_to_all | solution.py:80
  66.6 13.5 %all-to-all-start.3 = ((bf16[64,4,2,512]{3,2,0,1:T(2,128)(2,1)}), bf16[64,4,2,512]{3,2,0,1:T(2,128)(2,1)S(1)}, u32[]{:S(2)}, u32[]{:S(2)}) async-start(bf16[64,4,2,512]{3,2,0,1:T(2,128)(2,1)} %copy.146), calls=%async_computation.3 | async-start | bytes 1048576 | tf_op jit(solution)/shard_map/all_to_all | solution.py:79
  70.0 349.4 %all-reduce.7.cloned.1.call-start = ((), (), s32[]{:S(2)}) async-start(), calls=%async_computation.6 | async-start | bytes 11534336 | tf_op jit(solution)/shard_map/psum | solution.py:119
  89.9 1.4 copy-start.7
  96.5 4.9 %copy-start.8 = (bf16[64,4,8,128]{3,2,1,0:T(8,128)(2,1)S(1)}, bf16[64,4,8,128]{3,2,1,0:T(8,128)(2,1)}, u32[]{:S(2)}) copy-start(bf16[64,4,8,128]{3,2,1,0:T(8,128)(2,1)} %get-tuple-element.46) | copy-start | bytes 1572868
  101.3 2.6 copy-start.2
  115.3 5.1 %copy-start.10 = (bf16[512,512]{0,1:T(8,128)(2,1)S(1)}, bf16[512,512]{0,1:T(8,128)(2,1)}, u32[]{:S(2)}) copy-start(bf16[512,512]{0,1:T(8,128)(2,1)} %copy.176) | copy-start | bytes 1572868
  115.3 6.3 %copy-start.11 = (bf16[512,512]{0,1:T(8,128)(2,1)S(1)}, bf16[512,512]{0,1:T(8,128)(2,1)}, u32[]{:S(2)}) copy-start(bf16[512,512]{0,1:T(8,128)(2,1)} %copy.177) | copy-start | bytes 1572868
  120.4 2.9 copy-start.3
  120.4 2.9 copy-start.13
  137.8 1.3 copy-start.17
  137.8 1.6 copy-start.9
  137.8 4.0 copy-start.5
  141.8 1.5 copy-start.20
  143.3 35.9 %copy-start.6 = (bf16[512,512]{1,0:T(8,128)(2,1)S(1)}, bf16[512,512]{1,0:T(8,128)(2,1)}, u32[]{:S(2)}) copy-start(bf16[512,512]{1,0:T(8,128)(2,1)} %get-tuple-element.45) | copy-start | bytes 1572868
  147.9 24.7 %all-to-all-start.4 = ((bf16[64,4,2,512]{3,2,1,0:T(2,128)(2,1)}), bf16[64,4,2,512]{3,2,1,0:T(2,128)(2,1)}, u32[]{:S(2)}, u32[]{:S(2)}) async-start(bf16[64,4,2,512]{3,2,1,0:T(2,128)(2,1)} %reshape.212), calls=%async_computation.4 | async-start | bytes 1048576 | tf_op jit(solution)/shard_map/all_to_all | solution.py:91
  174.8 14.1 %all-to-all-start.5 = ((bf16[64,4,2,512]{3,2,0,1:T(2,128)(2,1)}), bf16[64,4,2,512]{3,2,0,1:T(2,128)(2,1)}, u32[]{:S(2)}, u32[]{:S(2)}) async-start(bf16[64,4,2,512]{3,2,0,1:T(2,128)(2,1)} %copy.164), calls=%async_computation.5 | async-start | bytes 1048576 | tf_op jit(solution)/shard_map/all_to_all | solution.py:90
  419.4 4.9 %copy-start.14 = (f32[512,512]{1,0:T(8,128)S(1)}, f32[512,512]{1,0:T(8,128)}, u32[]{:S(2)}) copy-start(f32[512,512]{1,0:T(8,128)} %get-tuple-element.42) | copy-start | bytes 3145732
  419.4 6.0 %copy-start.15 = (f32[256,512]{1,0:T(8,128)S(1)}, f32[256,512]{1,0:T(8,128)}, u32[]{:S(2)}) copy-start(f32[256,512]{1,0:T(8,128)} %get-tuple-element.40) | copy-start | bytes 1572868
  (3 other events, 2.3 us)
Sparse Core Ops, SparseCore 0:
  143.4 275.9 all-reduce.6
where the time goes:
time: 434 us; the launch traced here: 433 us
  waiting for transfers between devices  267 us (62%)
  local copies, waits for them, and re-layouts  40.3 us (9%)
  matrix products  37.4 us (9%)
  blocking collectives  26.2 us (6%)
  other arithmetic  24 us (6%)
  starting transfers between devices  23.4 us (5%)
  between operations  14.4 us (3%)
    psum x1, waiting for transfers between devices, on_device(): lax.psum((d_leaf.astype(jnp.float32), d_in.astype(jnp.float32), d_out.ast...  222 us
    all_to_all x1, blocking collectives, send_asked(): lax.all_to_all(wanted, 'dp', split_axis=0, concat_axis=0, tiled=True)  18.3 us
    all_to_all x1, waiting for transfers between devices, send_returned(): lax.all_to_all(gradients, 'dp', split_axis=0, concat_axis=0, tiled=True)  17.6 us
    all_to_all x1, waiting for transfers between devices, send_fetched(): lax.all_to_all(fetched, 'dp', split_axis=0, concat_axis=0, tiled=True)  15.3 us
  transfers between devices with their start and end apart: 5, of which 5 were waited for; matrix products, arithmetic and copies ran while one was open for 6% of the time, Pallas kernels for 0%

commit v1 on v0

--- a/solution.py
+++ b/solution.py
@@ -117,8 +117,10 @@
     d_rows, d_leaf, d_in = pull_front((d_inputs, d_gated))
     returned = send_returned(d_rows.reshape(data_count, replica_count, -1, width))
     leaf_sum, in_sum, out_sum = lax.psum(
-        (d_leaf.astype(jnp.float32), d_in.astype(jnp.float32), d_out.astype(jnp.float32)),
-        ("dp", "rep"),
+        lax.psum(
+            (d_leaf.astype(jnp.float32), d_in.astype(jnp.float32), d_out.astype(jnp.float32)), "rep"
+        ),
+        "dp",
     )
     table_grad = (
         jnp.zeros(item_table.shape, jnp.float32)

time: 434 us -> 492 us (1.13)
  waiting for transfers between devices: 267 us -> 318 us
    psum x0 -> x1, waiting for transfers between devices: none -> 155 us  [on_device(): lax.psum(lax.psum((d_leaf.astype(jnp.float32), d_in.astype(jnp.float32),...]
    psum x1, waiting for transfers between devices: 222 us -> 119 us  [on_device(): lax.psum((d_leaf.astype(jnp.float32), d_in.astype(jnp.float32), d_out.ast...]
  transfers between devices with their start and end apart: 5 -> 6, of which waited for: 5 -> 6; matrix products, arithmetic and copies ran while one was open for 6% -> 5% of each run, Pallas kernels for 0% -> 0%
where the time goes in v1:
time: 492 us; the launch traced here: 491 us
  waiting for transfers between devices  318 us (65%)
  local copies, waits for them, and re-layouts  43.3 us (9%)
  matrix products  37.4 us (8%)
  starting transfers between devices  27.5 us (6%)
  blocking collectives  26.2 us (5%)
  other arithmetic  23.4 us (5%)
  between operations  14.4 us (3%)
    psum x1, waiting for transfers between devices, on_device(): lax.psum(lax.psum((d_leaf.astype(jnp.float32), d_in.astype(jnp.float32),...  155 us
    psum x1, waiting for transfers between devices, on_device(): lax.psum((d_leaf.astype(jnp.float32), d_in.astype(jnp.float32), d_out.ast...  119 us
    all_to_all x1, blocking collectives, send_asked(): lax.all_to_all(wanted, 'dp', split_axis=0, concat_axis=0, tiled=True)  18.3 us
    all_to_all x1, waiting for transfers between devices, send_returned(): lax.all_to_all(gradients, 'dp', split_axis=0, concat_axis=0, tiled=True)  17.5 us
    all_to_all x1, waiting for transfers between devices, send_fetched(): lax.all_to_all(fetched, 'dp', split_axis=0, concat_axis=0, tiled=True)  15.3 us
    all_to_all x1, starting transfers between devices, send_returned(): lax.all_to_all(gradients, 'dp', split_axis=0, concat_axis=0, tiled=True)  10.8 us
  transfers between devices with their start and end apart: 6, of which 6 were waited for; matrix products, arithmetic and copies ran while one was open for 5% of the time, Pallas kernels for 0%

profile of v1, /device:TPU:97, one launch (start us, length us, event | category | flops | bytes accessed | tf_op | source)
XLA Modules:
  0.0 490.6 jit_solution(18214806253786493909)
XLA Ops:
  8.2 18.3 %all_to_all.30 = s32[64,4,2]{1,2,0:T(2,128)S(1)} all-to-all(s32[64,4,2]{1,2,0:T(2,128)S(1)} %copy.143), channel_id=1, replica_groups=mesh['dp'=64,'rep'=4] {'dp'}, dimensions={0} | all-to-all | bytes 4096 | tf_op jit(solution)/shard_map/all_to_all | solution.py:69
  26.7 7.9 %all_to_all.31 = s32[4,1,128]{2,1,0:T(1,128)S(1)} all-to-all(s32[4,1,128]{2,1,0:T(1,128)S(1)} %reshape.234), channel_id=1, replica_groups=mesh['dp'=64,'rep'=4] {'rep'}, dimensions={0} | all-to-all | bytes 4096 | tf_op jit(solution)/shard_map/all_to_all | solution.py:68
  36.2 3.6 gather_fusion
  41.8 8.5 %all-to-all-start.2 = ((bf16[64,4,2,512]{3,2,1,0:T(2,128)(2,1)}), bf16[64,4,2,512]{3,2,1,0:T(2,128)(2,1)S(1)}, u32[]{:S(2)}, u32[]{:S(2)}) async-start(bf16[64,4,2,512]{3,2,1,0:T(2,128)(2,1)} %reshape.215), calls=%async_computation.2 | async-start | bytes 1048576 | tf_op jit(solution)/shard_map/all_to_all | solution.py:80
  51.8 15.3 %all-to-all-done.2 = bf16[64,4,2,512]{3,2,1,0:T(2,128)(2,1)S(1)} async-done(((bf16[64,4,2,512]{3,2,1,0:T(2,128)(2,1)}), bf16[64,4,2,512]{3,2,1,0:T(2,128)(2,1)S(1)}, u32[]{:S(2)}, u32[]{:S(2)}) %all-to-all-start.2) | async-done | bytes 524320 | tf_op jit(solution)/shard_map/all_to_all | solution.py:80
  68.3 3.5 all-to-all-start.3
  74.5 7.3 %all-to-all-done.3 = bf16[64,4,2,512]{3,2,0,1:T(2,128)(2,1)S(1)} async-done(((bf16[64,4,2,512]{3,2,0,1:T(2,128)(2,1)}), bf16[64,4,2,512]{3,2,0,1:T(2,128)(2,1)S(1)}, u32[]{:S(2)}, u32[]{:S(2)}) %all-to-all-start.3) | async-done | bytes 524320 | tf_op jit(solution)/shard_map/all_to_all | solution.py:79
  87.8 3.8 multiply_convert_fusion
  98.3 4.9 select_convert_fusion
  105.7 2.6 copy.171
  111.1 3.0 fusion.40
  117.1 5.1 %fusion.4 = bf16[4,512,512]{2,1,0:T(8,128)(2,1)S(1)} fusion(f32[4,512,512]{2,1,0:T(8,128)} %get-tuple-element.60, pred[512,512]{1,0:T(8,128)(4,1)S(1)} %fusion.22, bf16[4,128,512]{2,1,0:T(8,128)(2,1)} %bitcast.72, bf16[64,4,8,128]{3,2,1,0:T(8,128)(2,1)} %get-tuple-element.49), kind=kOutput, calls=%fused_computation.10 | convolution fusion | flops 283115520 | bytes 7602176 | tf_op jit(solution)/shard_map/transpose(jvp(hqk,khd->qhd))/dot_general | solution.py:54
  132.7 3.6 fusion
  136.3 3.3 fusion.5
  145.1 119.4 %all-reduce.11.cloned.1.call-done = (f32[256,512]{1,0:T(8,128)}, f32[512,2048]{1,0:T(8,128)}, f32[512,512]{1,0:T(8,128)}) async-done(((f32[256,512]{1,0:T(8,128)}, f32[512,2048]{1,0:T(8,128)}, f32[512,512]{1,0:T(8,128)}), (f32[256,512]{1,0:T(8,128)}, f32[512,2048]{1,0:T(8,128)}, f32[512,512]{1,0:T(8,128)})) %all-reduce.11.cloned.1.call-update) | async-done | bytes 5767184 | tf_op jit(solution)/shard_map/psum | solution.py:120
  264.5 2.5 convolution_convert_fusion.1
  269.1 10.8 %all-to-all-start.4 = ((bf16[64,4,2,512]{3,2,1,0:T(2,128)(2,1)}), bf16[64,4,2,512]{3,2,1,0:T(2,128)(2,1)}, u32[]{:S(2)}, u32[]{:S(2)}) async-start(bf16[64,4,2,512]{3,2,1,0:T(2,128)(2,1)} %reshape.212), calls=%async_computation.4 | async-start | bytes 1048576 | tf_op jit(solution)/shard_map/all_to_all | solution.py:91
  280.3 17.5 %all-to-all-done.4 = bf16[64,4,2,512]{3,2,1,0:T(2,128)(2,1)} async-done(((bf16[64,4,2,512]{3,2,1,0:T(2,128)(2,1)}), bf16[64,4,2,512]{3,2,1,0:T(2,128)(2,1)}, u32[]{:S(2)}, u32[]{:S(2)}) %all-to-all-start.4) | async-done | bytes 524320 | tf_op jit(solution)/shard_map/all_to_all | solution.py:91
  299.9 4.4 all-to-all-start.5
  304.3 2.3 fusion.11
  308.7 4.1 all-to-all-done.5
  317.8 4.2 scatter_custom_fusion
  322.1 154.9 %all-reduce.9.cloned.1.call-done = (f32[256,512]{1,0:T(8,128)}, f32[512,2048]{1,0:T(8,128)}, f32[512,512]{1,0:T(8,128)}) async-done(((f32[256,512]{1,0:T(8,128)}, f32[512,2048]{1,0:T(8,128)}, f32[512,512]{1,0:T(8,128)}), (f32[256,512]{1,0:T(8,128)}, f32[512,2048]{1,0:T(8,128)}, f32[512,512]{1,0:T(8,128)})) %all-reduce.9.cloned.1.call-update) | async-done | bytes 5767184 | tf_op jit(solution)/shard_map/psum | solution.py:119
  477.0 4.9 %broadcast_multiply_fusion = f32[512,2048]{1,0:T(8,128)} fusion(f32[512,2048]{1,0:T(8,128)} %get-tuple-element.41), kind=kLoop, calls=%fused_computation.17 | loop fusion | flops 1048576 | bytes 8388608 | tf_op jit(solution)/shard_map/mul | solution.py:131
  (110 shorter events, 60.6 us)
Async XLA Ops:
  7.2 80.6 %copy-start = (bf16[512,2048]{1,0:T(8,128)(2,1)S(1)}, bf16[512,2048]{1,0:T(8,128)(2,1)}, u32[]{:S(2)}) copy-start(bf16[512,2048]{1,0:T(8,128)(2,1)} %param.15) | copy-start | bytes 6291460
  7.2 43.2 %copy-start.21 = (s32[1,4]{1,0:T(1,128)S(1)}, s32[1,4]{1,0:T(1,128)}, u32[]{:S(2)}) copy-start(s32[1,4]{1,0:T(1,128)} %param.12) | copy-start | bytes 52
  7.2 43.4 %copy-start.4 = (bf16[512,512]{1,0:T(8,128)(2,1)S(1)}, bf16[512,512]{1,0:T(8,128)(2,1)}, u32[]{:S(2)}) copy-start(bf16[512,512]{1,0:T(8,128)(2,1)} %param.17) | copy-start | bytes 1572868
  26.5 25.1 %copy-start.18 = (s32[512,8]{0,1:T(8,128)S(1)}, s32[512,8]{0,1:T(8,128)}, u32[]{:S(2)}) copy-start(s32[512,8]{0,1:T(8,128)} %param.13) | copy-start | bytes 49156
  41.8 43.1 %copy-start.19 = (s32[512]{0:T(512)S(1)}, s32[512]{0:T(512)}, u32[]{:S(2)}) copy-start(s32[512]{0:T(512)} %param.11) | copy-start | bytes 6148
  41.8 25.3 %all-to-all-start.2 = ((bf16[64,4,2,512]{3,2,1,0:T(2,128)(2,1)}), bf16[64,4,2,512]{3,2,1,0:T(2,128)(2,1)S(1)}, u32[]{:S(2)}, u32[]{:S(2)}) async-start(bf16[64,4,2,512]{3,2,1,0:T(2,128)(2,1)} %reshape.215), calls=%async_computation.2 | async-start | bytes 1048576 | tf_op jit(solution)/shard_map/all_to_all | solution.py:80
  68.3 13.5 %all-to-all-start.3 = ((bf16[64,4,2,512]{3,2,0,1:T(2,128)(2,1)}), bf16[64,4,2,512]{3,2,0,1:T(2,128)(2,1)S(1)}, u32[]{:S(2)}, u32[]{:S(2)}) async-start(bf16[64,4,2,512]{3,2,0,1:T(2,128)(2,1)} %copy.146), calls=%async_computation.3 | async-start | bytes 1048576 | tf_op jit(solution)/shard_map/all_to_all | solution.py:79
  71.7 192.7 %all-reduce.11.cloned.1.call-start = ((), (), s32[]{:S(2)}) async-start(), calls=%async_computation.7 | async-start | bytes 11534336 | tf_op jit(solution)/shard_map/psum | solution.py:120
  91.6 1.4 copy-start.7
  98.3 4.9 copy-start.8
  103.1 2.6 copy-start.2
  117.1 5.1 %copy-start.10 = (bf16[512,512]{0,1:T(8,128)(2,1)S(1)}, bf16[512,512]{0,1:T(8,128)(2,1)}, u32[]{:S(2)}) copy-start(bf16[512,512]{0,1:T(8,128)(2,1)} %copy.176) | copy-start | bytes 1572868
  117.1 6.3 %copy-start.11 = (bf16[512,512]{0,1:T(8,128)(2,1)S(1)}, bf16[512,512]{0,1:T(8,128)(2,1)}, u32[]{:S(2)}) copy-start(bf16[512,512]{0,1:T(8,128)(2,1)} %copy.177) | copy-start | bytes 1572868
  122.1 2.9 copy-start.3
  122.2 2.9 copy-start.13
  139.6 1.6 copy-start.9
  139.6 3.9 copy-start.5
  145.0 119.5 %copy-start.20 = (s32[512]{0:T(512)S(1)}, s32[512]{0:T(512)}, u32[]{:S(2)}) copy-start(s32[512]{0:T(512)} %param.11) | copy-start | bytes 6148
  145.0 331.9 %all-reduce.9.cloned.1.call-start = ((), (), s32[]{:S(2)}) async-start(), calls=%async_computation.6 | async-start | bytes 11534336 | tf_op jit(solution)/shard_map/psum | solution.py:119
  264.5 39.8 %copy-start.6 = (bf16[512,512]{1,0:T(8,128)(2,1)S(1)}, bf16[512,512]{1,0:T(8,128)(2,1)}, u32[]{:S(2)}) copy-start(bf16[512,512]{1,0:T(8,128)(2,1)} %get-tuple-element.48) | copy-start | bytes 1572868
  269.1 28.6 %all-to-all-start.4 = ((bf16[64,4,2,512]{3,2,1,0:T(2,128)(2,1)}), bf16[64,4,2,512]{3,2,1,0:T(2,128)(2,1)}, u32[]{:S(2)}, u32[]{:S(2)}) async-start(bf16[64,4,2,512]{3,2,1,0:T(2,128)(2,1)} %reshape.212), calls=%async_computation.4 | async-start | bytes 1048576 | tf_op jit(solution)/shard_map/all_to_all | solution.py:91
  299.9 13.0 %all-to-all-start.5 = ((bf16[64,4,2,512]{3,2,0,1:T(2,128)(2,1)}), bf16[64,4,2,512]{3,2,0,1:T(2,128)(2,1)}, u32[]{:S(2)}, u32[]{:S(2)}) async-start(bf16[64,4,2,512]{3,2,0,1:T(2,128)(2,1)} %copy.164), calls=%async_computation.5 | async-start | bytes 1048576 | tf_op jit(solution)/shard_map/all_to_all | solution.py:90
  477.0 4.9 %copy-start.14 = (f32[512,512]{1,0:T(8,128)S(1)}, f32[512,512]{1,0:T(8,128)}, u32[]{:S(2)}) copy-start(f32[512,512]{1,0:T(8,128)} %get-tuple-element.42) | copy-start | bytes 3145732
  477.0 6.0 %copy-start.15 = (f32[256,512]{1,0:T(8,128)S(1)}, f32[256,512]{1,0:T(8,128)}, u32[]{:S(2)}) copy-start(f32[256,512]{1,0:T(8,128)} %get-tuple-element.40) | copy-start | bytes 1572868
  (4 other events, 3.7 us)
Sparse Core Ops, SparseCore 0:
  145.2 119.2 all-reduce.10
  268.4 208.5 all-reduce.8
